TPU v7x, 32 devices: a whole 2x2x4 slice. The times are simulated.
32 devices in a mesh: expert: 8 (over z, y), hidden: 4 (over x, core).
Axes of the slice: x: 2, y: 2, z: 4, core: 2. Of those that a mesh axis runs over, the one named last changes fastest.
Arguments:
- tokens: bfloat16 [2, 6144, 768], P(None, 'expert'), may hold values from -6 to 6
- doc_ids: int32 [2, 8, 768], P(None, 'expert'), may hold values from 0 to 3, never falling along the last dimension, each value on 1 to 384 neighbouring positions
- pad_mask: int32 [2, 6144], P(None, 'expert'), may hold values 0 or 1
- norm1_gain: float32 [768], replicated, may hold values from 0.5 to 1.5
- norm1_bias: float32 [768], replicated, may hold values from -1 to 1
- qkv_weight: bfloat16 [3, 768, 768], P(None, None, 'hidden'), may hold values from -0.3125 to 0.3125
- out_weight: bfloat16 [768, 768], P('hidden'), may hold values from -0.875 to 0.875
- norm2_gain: float32 [768], replicated, may hold values from 0.5 to 1.5
- norm2_bias: float32 [768], replicated, may hold values from -1 to 1
- router: bfloat16 [768, 8], replicated, may hold values from -0.15625 to 0.15625
- routes: int32 [2, 6144, 2], P(None, 'expert'), may hold values from 0 to 7, all different within a row; in each aligned block of 768 rows (0 to 767, 768 to 1535, ..., all dimensions but the last counted through in order) at most 384 rows name the same one
- up_weight: bfloat16 [8, 768, 3072], P('expert', None, 'hidden'), may hold values from -0.21875 to 0.21875
- down_weight: bfloat16 [8, 768, 3072], P('expert', None, 'hidden'), may hold values from -0.15625 to 0.15625
- cotangent: bfloat16 [2, 6144, 768], P(None, 'expert'), may hold values from -6 to 6
Outputs:
- block_out: float32 [2, 6144, 768], P(None, 'expert')
- grad_tokens: float32 [2, 6144, 768], P(None, 'expert')
- grad_norm1_gain: float32 [768], replicated
- grad_norm1_bias: float32 [768], replicated
- grad_qkv: float32 [3, 768, 768], P(None, None, 'hidden')
- grad_out: float32 [768, 768], P('hidden')
- grad_norm2_gain: float32 [768], replicated
- grad_norm2_bias: float32 [768], replicated
- grad_router: float32 [768, 8], replicated
- grad_up: float32 [4, 768, 3072], P(None, 'expert', 'hidden')
- grad_down: float32 [4, 768, 3072], P(None, 'expert', 'hidden')
Inputs may be any that keep to these rules, and one draw needn't show every extreme that they name: `routes`: each token names 2 different experts. In each micro-batch the tokens of one pack name any one expert at most 384 times, a bound that some block reaches. `doc_ids`: within a pack document numbers never fall; each document covers 1 to 384 consecutive tokens, and some covers exactly 384. `pad_mask`: 1 marks a real token, 0 a padding token.
All inputs are finite; a program needn't handle non-finite values. No bound on the sum of `pad_mask` on one device may be relied on, other than what follows from the above.
Results may differ from a plain program's by a relative error of at most 0.028.
Values may be sent and summed in bfloat16 or wider, within the bound.
No kernel may reach another device: no remote copies, remote signals or barrier semaphores. Data moves between devices by JAX's collectives and lax.ppermute only.
A program may use at most 256 MiB of HBM per device.

v0:
```python
import jax
import jax.numpy as jnp
from jax import lax
from jax.sharding import PartitionSpec as P

HEAD_DIM = 64
EPSILON = 1e-05
PRECISE = lax.Precision.HIGHEST
MASKED = -1e30


def layer_norm(values, norm_gain, norm_bias):
    centre = values - jnp.mean(values, -1, keepdims=True)
    spread = jnp.mean(centre * centre, -1, keepdims=True)
    return centre * lax.rsqrt(spread + EPSILON) * norm_gain + norm_bias


def gelu_tanh(values):
    return jax.nn.gelu(values, approximate=True)


def visible(doc_row, pad_row):
    total_rows = doc_row.shape[0]
    query_pos = jnp.arange(total_rows)[:, None]
    key_pos = jnp.arange(total_rows)[None, :]
    same_doc = doc_row[:, None] == doc_row[None, :]
    is_real = (pad_row[None, :] == 1) | (query_pos == key_pos)
    return (key_pos <= query_pos) & same_doc & is_real


def slot_tables(route_rows, experts, capacity):
    flat_routes = route_rows.reshape(-1)
    onehot = (flat_routes[:, None] == jnp.arange(experts, dtype=jnp.int32)[None, :]).astype(
        jnp.int32
    )
    before = jnp.cumsum(onehot, 0) - onehot
    placed = jnp.sum(before * onehot, 1)
    slot_index = flat_routes * capacity + placed
    total_rows = flat_routes.shape[0]
    source = (
        jnp.full((experts * capacity,), total_rows, jnp.int32)
        .at[slot_index]
        .set(jnp.arange(total_rows, dtype=jnp.int32))
    )
    return (slot_index, source)


def masked_scores(queries, key_rows, allowed, score_scale):
    scores = (
        jnp.einsum("qhd,khd->hqk", queries, key_rows, preferred_element_type=jnp.float32)
        * score_scale
    )
    return jnp.where(allowed[None], scores, MASKED)


def attend_forward(queries, key_rows, value_rows, allowed, score_scale):
    scores = masked_scores(queries, key_rows, allowed, score_scale)
    row_peak = jnp.max(scores, -1, keepdims=True)
    exponent = jnp.exp(scores - row_peak)
    row_total = jnp.sum(exponent, -1, keepdims=True)
    attn_weights = (exponent / row_total).astype(jnp.bfloat16)
    output = jnp.einsum(
        "hqk,khd->qhd", attn_weights, value_rows, preferred_element_type=jnp.float32
    )
    return (output, row_peak + jnp.log(row_total))


def attend_backward(queries, key_rows, value_rows, allowed, score_scale, log_total, heads_grad):
    scores = masked_scores(queries, key_rows, allowed, score_scale)
    attn_weights = jnp.exp(scores - log_total)
    weight_grad = jnp.einsum(
        "qhd,khd->hqk", heads_grad, value_rows, preferred_element_type=jnp.float32
    )
    row_delta = jnp.sum(attn_weights * weight_grad, -1, keepdims=True)
    score_grad = (attn_weights * (weight_grad - row_delta)).astype(jnp.bfloat16)
    query_grad = (
        jnp.einsum("hqk,khd->qhd", score_grad, key_rows, preferred_element_type=jnp.float32)
        * score_scale
    )
    key_grad = (
        jnp.einsum("hqk,qhd->khd", score_grad, queries, preferred_element_type=jnp.float32)
        * score_scale
    )
    value_grad = jnp.einsum(
        "hqk,qhd->khd",
        attn_weights.astype(jnp.bfloat16),
        heads_grad,
        preferred_element_type=jnp.float32,
    )
    return (query_grad, key_grad, value_grad)


def shards(
    tokens,
    doc_ids,
    pad_mask,
    norm1_gain,
    norm1_bias,
    qkv_weight,
    out_weight,
    norm2_gain,
    norm2_bias,
    router,
    routes,
    up_weight,
    down_weight,
    cotangent,
):
    micro_count, row_count, feat_width = tokens.shape
    expert_count = router.shape[1]
    top_count = routes.shape[2]
    capacity = 2 * row_count * top_count // expert_count
    local_heads = qkv_weight.shape[2] // HEAD_DIM
    score_scale = HEAD_DIM ** (-0.5)
    trainable = lax.axis_index("expert") >= lax.axis_size("expert") // 2
    up_local = up_weight[0]
    down_local = down_weight[0]
    router_wide = router.astype(jnp.float32)
    zero_row = jnp.zeros((1, feat_width), jnp.bfloat16)
    grad_qkv = jnp.zeros(qkv_weight.shape, jnp.float32)
    grad_proj = jnp.zeros(out_weight.shape, jnp.float32)
    grad_router = jnp.zeros(router.shape, jnp.float32)
    gain1_total = jnp.zeros((feat_width,), jnp.float32)
    bias1_total = jnp.zeros((feat_width,), jnp.float32)
    gain2_total = jnp.zeros((feat_width,), jnp.float32)
    bias2_total = jnp.zeros((feat_width,), jnp.float32)
    expert_acc = (jnp.zeros(up_local.shape, jnp.float32), jnp.zeros(down_local.shape, jnp.float32))
    outputs = []
    input_grads = []
    for micro_idx in range(micro_count):
        inputs = tokens[micro_idx].astype(jnp.float32)
        allowed = visible(doc_ids[micro_idx, 0], pad_mask[micro_idx])
        normed1, norm1_pull = jax.vjp(layer_norm, inputs, norm1_gain, norm1_bias)
        attn_in = normed1.astype(jnp.bfloat16)
        projected = jnp.einsum(
            "rd,cdf->crf", attn_in, qkv_weight, preferred_element_type=jnp.float32
        ).astype(jnp.bfloat16)
        head_view = projected.reshape(3, row_count, local_heads, HEAD_DIM)
        queries, key_rows, value_rows = (head_view[0], head_view[1], head_view[2])
        heads_out, log_total = attend_forward(queries, key_rows, value_rows, allowed, score_scale)
        heads_low = heads_out.reshape(row_count, -1).astype(jnp.bfloat16)
        attn_term = jnp.dot(heads_low, out_weight, preferred_element_type=jnp.float32)
        attention = lax.psum(attn_term.astype(jnp.bfloat16), "hidden").astype(jnp.float32)
        residual = inputs + attention
        normed2, norm2_pull = jax.vjp(layer_norm, residual, norm2_gain, norm2_bias)
        moe_in = normed2.astype(jnp.bfloat16)
        logits = jnp.dot(moe_in, router, preferred_element_type=jnp.float32)
        route_rows = routes[micro_idx]
        picker = (
            route_rows[:, :, None] == jnp.arange(expert_count, dtype=jnp.int32)[None, None, :]
        ).astype(jnp.float32)
        chosen = jnp.sum(picker * logits[:, None, :], -1)
        gate_vals = jax.nn.softmax(chosen, -1)
        slot_index, source = slot_tables(route_rows, expert_count, capacity)
        padded_in = jnp.concatenate([moe_in, zero_row], 0)
        send_rows = padded_in[source // top_count].reshape(expert_count, capacity, feat_width)
        received = lax.all_to_all(
            send_rows, "expert", split_axis=0, concat_axis=0, tiled=True
        ).reshape(-1, feat_width)
        hidden_pre = jnp.dot(received, up_local, preferred_element_type=jnp.float32)
        hidden_act = gelu_tanh(hidden_pre).astype(jnp.bfloat16)
        slice_out = jnp.einsum(
            "rf,df->rd", hidden_act, down_local, preferred_element_type=jnp.float32
        )
        summed = lax.psum(slice_out.astype(jnp.bfloat16), "hidden")
        returned = lax.all_to_all(
            summed.reshape(expert_count, capacity, feat_width),
            "expert",
            split_axis=0,
            concat_axis=0,
            tiled=True,
        )
        flat_back = jnp.concatenate([returned.reshape(-1, feat_width), zero_row], 0)
        expert_rows = flat_back[slot_index].reshape(row_count, top_count, feat_width)
        expert_wide = expert_rows.astype(jnp.float32)
        mixture = jnp.sum(gate_vals[:, :, None] * expert_wide, 1)
        outputs.append(residual + mixture)
        upstream = cotangent[micro_idx].astype(jnp.float32)
        expert_grad = (gate_vals[:, :, None] * upstream[:, None, :]).astype(jnp.bfloat16)
        gate_grad = jnp.sum(upstream[:, None, :] * expert_wide, -1)
        chosen_grad = gate_vals * (gate_grad - jnp.sum(gate_vals * gate_grad, -1, keepdims=True))
        logit_grad = jnp.sum(picker * chosen_grad[:, :, None], 1)
        padded_grad = jnp.concatenate([expert_grad.reshape(-1, feat_width), zero_row], 0)
        send_grad = padded_grad[source].reshape(expert_count, capacity, feat_width)
        grad_rows = lax.all_to_all(
            send_grad, "expert", split_axis=0, concat_axis=0, tiled=True
        ).reshape(-1, feat_width)
        act_grad = jnp.dot(grad_rows, down_local, preferred_element_type=jnp.float32)
        gelu_grad = jax.vjp(gelu_tanh, hidden_pre)[1](act_grad)[0]
        pre_grad = gelu_grad.astype(jnp.bfloat16)
        in_term = jnp.einsum("rf,df->rd", pre_grad, up_local, preferred_element_type=jnp.float32)
        in_summed = lax.psum(in_term.astype(jnp.bfloat16), "hidden")
        in_back = lax.all_to_all(
            in_summed.reshape(expert_count, capacity, feat_width),
            "expert",
            split_axis=0,
            concat_axis=0,
            tiled=True,
        )
        flat_in = jnp.concatenate([in_back.reshape(-1, feat_width), zero_row], 0)
        copies_low = flat_in[slot_index].reshape(row_count, top_count, feat_width)
        copies_grad = copies_low.astype(jnp.float32)
        normed2_grad = jnp.sum(copies_grad, 1) + jnp.dot(
            logit_grad, router_wide.T, precision=PRECISE
        )

        def expert_update(acc_pair):
            return (
                acc_pair[0]
                + jnp.einsum("rd,rf->df", received, pre_grad, preferred_element_type=jnp.float32),
                acc_pair[1]
                + jnp.einsum(
                    "rd,rf->df", grad_rows, hidden_act, preferred_element_type=jnp.float32
                ),
            )

        def expert_keep(acc_pair):
            return acc_pair

        expert_acc = lax.cond(trainable, expert_update, expert_keep, expert_acc)
        grad_router = grad_router + jnp.dot(
            moe_in.astype(jnp.float32).T, logit_grad, precision=PRECISE
        )
        resid_grad, gain2_grad, bias2_grad = norm2_pull(normed2_grad)
        gain2_total = gain2_total + gain2_grad
        bias2_total = bias2_total + bias2_grad
        resid_grad = upstream + resid_grad
        attn_grad = resid_grad.astype(jnp.bfloat16)
        grad_proj = grad_proj + jnp.einsum(
            "rf,rd->fd", heads_low, attn_grad, preferred_element_type=jnp.float32
        )
        heads_grad = jnp.einsum(
            "rd,fd->rf", attn_grad, out_weight, preferred_element_type=jnp.float32
        ).astype(jnp.bfloat16)
        query_grad, key_grad, value_grad = attend_backward(
            queries,
            key_rows,
            value_rows,
            allowed,
            score_scale,
            log_total,
            heads_grad.reshape(row_count, local_heads, HEAD_DIM),
        )
        qkv_grad = (
            jnp.stack([query_grad, key_grad, value_grad])
            .reshape(3, row_count, -1)
            .astype(jnp.bfloat16)
        )
        grad_qkv = grad_qkv + jnp.einsum(
            "rd,crf->cdf", attn_in, qkv_grad, preferred_element_type=jnp.float32
        )
        normed1_term = jnp.einsum(
            "crf,cdf->rd", qkv_grad, qkv_weight, preferred_element_type=jnp.float32
        )
        normed1_grad = lax.psum(normed1_term.astype(jnp.bfloat16), "hidden").astype(jnp.float32)
        input_grad, gain1_grad, bias1_grad = norm1_pull(normed1_grad)
        gain1_total = gain1_total + gain1_grad
        bias1_total = bias1_total + bias1_grad
        input_grads.append(resid_grad + input_grad)
    reduced = (
        lax.psum(gain1_total.astype(jnp.bfloat16), "expert").astype(jnp.float32),
        lax.psum(bias1_total.astype(jnp.bfloat16), "expert").astype(jnp.float32),
        lax.psum(grad_qkv.astype(jnp.bfloat16), "expert").astype(jnp.float32),
        lax.psum(grad_proj.astype(jnp.bfloat16), "expert").astype(jnp.float32),
        lax.psum(gain2_total.astype(jnp.bfloat16), "expert").astype(jnp.float32),
        lax.psum(bias2_total.astype(jnp.bfloat16), "expert").astype(jnp.float32),
        lax.psum(grad_router.astype(jnp.bfloat16), "expert").astype(jnp.float32),
    )
    expert_parts = (
        lax.all_to_all(
            expert_acc[0][None].astype(jnp.bfloat16),
            "expert",
            split_axis=1,
            concat_axis=0,
            tiled=True,
        ).astype(jnp.float32),
        lax.all_to_all(
            expert_acc[1][None].astype(jnp.bfloat16),
            "expert",
            split_axis=1,
            concat_axis=0,
            tiled=True,
        ).astype(jnp.float32),
    )
    half_count = expert_count // 2
    return (
        jnp.stack(outputs),
        jnp.stack(input_grads),
        reduced[0],
        reduced[1],
        reduced[2],
        reduced[3],
        reduced[4],
        reduced[5],
        reduced[6],
        expert_parts[0][half_count:],
        expert_parts[1][half_count:],
    )


def solution(mesh):
    placed = (
        P(None, "expert", None),
        P(None, "expert", None),
        P(None, "expert"),
        P(),
        P(),
        P(None, None, "hidden"),
        P("hidden", None),
        P(),
        P(),
        P(),
        P(None, "expert", None),
        P("expert", None, "hidden"),
        P("expert", None, "hidden"),
        P(None, "expert", None),
    )
    return jax.shard_map(
        shards,
        mesh=mesh,
        in_specs=placed,
        out_specs=(
            P(None, "expert", None),
            P(None, "expert", None),
            P(),
            P(),
            P(None, None, "hidden"),
            P("hidden", None),
            P(),
            P(),
            P(),
            P(None, "expert", "hidden"),
            P(None, "expert", "hidden"),
        ),
        check_vma=False,
    )
```

profile of v0, /device:TPU:0, one launch (start us, length us, event | category | flops | bytes accessed | tf_op | source)
XLA Modules:
  0.0 1665.4 jit_solution(2692091185587568231)
XLA Ops:
  46.8 17.9 %all-reduce.18.cloned.1.call-done = bf16[768,768]{1,0:T(8,128)(2,1)} async-done(((bf16[768,768]{1,0:T(8,128)(2,1)}), bf16[768,768]{1,0:T(8,128)(2,1)}) %all-reduce.18.cloned.1.call-update) | async-done | bytes 1179664 | tf_op jit(solution)/shard_map/psum | solution.py:143
  128.2 14.5 gather_fusion.4
  159.9 14.5 gather_fusion.2
  174.4 78.2 %all-to-all-done.4 = bf16[8,384,768]{2,1,0:T(8,128)(2,1)} async-done(((bf16[8,384,768]{2,1,0:T(8,128)(2,1)}), bf16[8,384,768]{2,1,0:T(8,128)(2,1)}, u32[]{:S(2)}, u32[]{:S(2)}) %all-to-all-start.4) | async-done | bytes 4718624 | tf_op jit(solution)/shard_map/all_to_all | solution.py:185
  257.5 14.5 gather_fusion
  272.1 89.1 %all-to-all-done.2 = bf16[8,384,768]{2,1,0:T(8,128)(2,1)} async-done(((bf16[8,384,768]{2,1,0:T(8,128)(2,1)}), bf16[8,384,768]{2,1,0:T(8,128)(2,1)}, u32[]{:S(2)}, u32[]{:S(2)}) %all-to-all-start.2) | async-done | bytes 4718624 | tf_op jit(solution)/shard_map/all_to_all | solution.py:157
  382.2 14.6 gather_fusion.6
  396.8 72.8 %all-to-all-done = bf16[8,384,768]{2,1,0:T(8,128)(2,1)} async-done(((bf16[8,384,768]{2,1,0:T(8,128)(2,1)}), bf16[8,384,768]{2,1,0:T(8,128)(2,1)}, u32[]{:S(2)}, u32[]{:S(2)}) %all-to-all-start) | async-done | bytes 4718624 | tf_op jit(solution)/shard_map/all_to_all | solution.py:157
  482.1 12.1 fusion.6
  515.4 62.6 %all-to-all-done.6 = bf16[8,384,768]{2,1,0:T(8,128)(2,1)} async-done(((bf16[8,384,768]{2,1,0:T(8,128)(2,1)}), bf16[8,384,768]{2,1,0:T(8,128)(2,1)}, u32[]{:S(2)}, u32[]{:S(2)}) %all-to-all-start.6) | async-done | bytes 4718624 | tf_op jit(solution)/shard_map/all_to_all | solution.py:185
  578.0 11.9 fusion.13
  618.3 32.7 %all-to-all-start.8 = ((bf16[8,2,36864]{2,1,0:T(2,128)(2,1)}), bf16[8,2,36864]{2,1,0:T(2,128)(2,1)}, u32[]{:S(2)}, u32[]{:S(2)}) async-start(bf16[8,2,36864]{2,1,0:T(2,128)(2,1)} %reshape.916), calls=%async_computation.8 | async-start | bytes 2359296 | tf_op jit(solution)/shard_map/all_to_all | solution.py:270
  661.1 18.7 %all-to-all-done.8 = bf16[8,2,36864]{2,1,0:T(2,128)(2,1)} async-done(((bf16[8,2,36864]{2,1,0:T(2,128)(2,1)}), bf16[8,2,36864]{2,1,0:T(2,128)(2,1)}, u32[]{:S(2)}, u32[]{:S(2)}) %all-to-all-start.8) | async-done | bytes 1179680 | tf_op jit(solution)/shard_map/all_to_all | solution.py:270
  679.8 32.5 %all_to_all.58 = bf16[8,2,36864]{2,1,0:T(2,128)(2,1)S(1)} all-to-all(bf16[8,2,36864]{2,1,0:T(2,128)(2,1)S(1)} %reshape.918), channel_id=1, replica_groups=mesh['expert'=8,'hidden'=4] {'expert'}, dimensions={0} | all-to-all | bytes 2359296 | tf_op jit(solution)/shard_map/all_to_all | solution.py:277
  712.3 208.9 %all-reduce.26.cloned.1.call-done = (bf16[8,384,768]{2,1,0:T(8,128)(2,1)}, bf16[8,384,768]{2,1,0:T(8,128)(2,1)}, bf16[8,384,768]{2,1,0:T(8,128)(2,1)}, bf16[8,384,768]{2,1,0:T(8,128)(2,1)}) async-done(((bf16[8,384,768]{2,1,0:T(8,128)(2,1)}, bf16[8,384,768]{2,1,0:T(8,128)(2,1)}, bf16[8,384,768]{2,1,0:T(8,128)(2,1)}, bf16[8,384,768]{2,1,0:T(8,128)(2,1)}), (bf16[8,384,768]{2,1,0:T(8,128)(2,1)}, ...) | async-done | bytes 18874384 | tf_op jit(solution)/shard_map/psum | solution.py:165
  921.3 110.1 %all_to_all.59 = bf16[8,384,768]{2,1,0:T(8,128)(2,1)} all-to-all(bf16[8,384,768]{2,1,0:T(8,128)(2,1)} %get-tuple-element.99), channel_id=1, replica_groups=mesh['expert'=8,'hidden'=4] {'expert'}, dimensions={0} | all-to-all | bytes 9437184 | tf_op jit(solution)/shard_map/all_to_all | solution.py:166
  1031.4 107.6 %all_to_all.60 = bf16[8,384,768]{2,1,0:T(8,128)(2,1)} all-to-all(bf16[8,384,768]{2,1,0:T(8,128)(2,1)S(1)} %copy-done.38), channel_id=1, replica_groups=mesh['expert'=8,'hidden'=4] {'expert'}, dimensions={0} | all-to-all | bytes 9437184 | tf_op jit(solution)/shard_map/all_to_all | solution.py:193
  1139.0 107.5 %all_to_all.61 = bf16[8,384,768]{2,1,0:T(8,128)(2,1)} all-to-all(bf16[8,384,768]{2,1,0:T(8,128)(2,1)S(1)} %bitcast.379), channel_id=1, replica_groups=mesh['expert'=8,'hidden'=4] {'expert'}, dimensions={0} | all-to-all | bytes 9437184 | tf_op jit(solution)/shard_map/all_to_all | solution.py:193
  1296.2 58.5 %all-to-all-done.3 = bf16[8,384,768]{2,1,0:T(8,128)(2,1)} async-done(((bf16[8,384,768]{2,1,0:T(8,128)(2,1)}), bf16[8,384,768]{2,1,0:T(8,128)(2,1)}, u32[]{:S(2)}, u32[]{:S(2)}) %all-to-all-start.3) | async-done | bytes 4718624 | tf_op jit(solution)/shard_map/all_to_all | solution.py:166
  1385.8 13.4 multiply_reduce_fusion.2
  1406.4 13.7 multiply_reduce_fusion.3
  1515.0 47.2 %all-reduce.24.cloned.1.call-done = (bf16[768,768]{1,0:T(8,128)(2,1)}, bf16[768,768]{1,0:T(8,128)(2,1)}) async-done(((bf16[768,768]{1,0:T(8,128)(2,1)}, bf16[768,768]{1,0:T(8,128)(2,1)}), (bf16[768,768]{1,0:T(8,128)(2,1)}, bf16[768,768]{1,0:T(8,128)(2,1)})) %all-reduce.24.cloned.1.call-update) | async-done | bytes 2359312 | tf_op jit(solution)/shard_map/psum | solution.py:255
  1570.1 38.8 %all-reduce.8 = (bf16[768]{0:T(1024)(128)(2,1)}, bf16[768]{0:T(1024)(128)(2,1)}, bf16[768]{0:T(1024)(128)(2,1)}, bf16[768]{0:T(1024)(128)(2,1)}, bf16[768,8]{0,1:T(8,128)(2,1)}) all-reduce(bf16[768]{0:T(1024)(128)(2,1)} %add_convert_fusion.6, ...), channel_id=1, replica_groups=mesh['expert'=8,'hidden'=4] {'expert'}, use_global_device_ids=true, to_apply=%region_56.57 | all-reduce | flops 9216 | bytes 36864 | tf_op jit(solution)/shard_map/psum | solution.py:261
  1617.8 29.0 %all-reduce.22.cloned.1.call-done = (bf16[3,768,192]{1,2,0:T(8,128)(2,1)}, bf16[192,768]{1,0:T(8,128)(2,1)}) async-done(((bf16[3,768,192]{1,2,0:T(8,128)(2,1)}, bf16[192,768]{1,0:T(8,128)(2,1)}), (bf16[3,768,192]{1,2,0:T(8,128)(2,1)}, bf16[192,768]{1,0:T(8,128)(2,1)})) %all-reduce.22.cloned.1.call-update) | async-done | bytes 1179664 | tf_op jit(solution)/shard_map/psum | solution.py:263
  (532 shorter events, 429.3 us)
Async XLA Ops:
  7.2 467.2 %copy-start = (bf16[1,768,768]{2,1,0:T(8,128)(2,1)S(1)}, bf16[1,768,768]{2,1,0:T(8,128)(2,1)}, u32[]{:S(2)}) copy-start(bf16[1,768,768]{2,1,0:T(8,128)(2,1)} %param.29) | copy-start | bytes 3538948
  7.2 57.4 %all-reduce.18.cloned.1.call-start = ((), (), s32[]{:S(2)}) async-start(), calls=%async_computation.10 | async-start | bytes 2359296 | tf_op jit(solution)/shard_map/psum | solution.py:143
  24.2 91.2 %all-reduce.20.cloned.1.call-start = ((), (), s32[]{:S(2)}) async-start(), calls=%async_computation.11 | async-start | bytes 2359296 | tf_op jit(solution)/shard_map/psum | solution.py:143
  26.0 97.0 %copy-start.102 = (s32[768,2]{0,1:T(2,128)}, s32[768,2]{0,1:T(2,128)S(1)}, u32[]{:S(2)}) copy-start(s32[768,2]{0,1:T(2,128)S(1)} %get-tuple-element.125) | copy-start | bytes 18436
  42.6 24.8 %copy-start.89 = (f32[768]{0:T(1024)}, f32[768]{0:T(1024)S(1)}, u32[]{:S(2)}) copy-start(f32[768]{0:T(1024)S(1)} %broadcast_multiply_fusion.3) | copy-start | bytes 9220
  88.1 17.2 %copy-start.138 = (f32[768]{0:T(1024)S(1)}, f32[768]{0:T(1024)}, u32[]{:S(2)}) copy-start(f32[768]{0:T(1024)} %get-tuple-element.75) | copy-start | bytes 9220
  142.7 110.0 %all-to-all-start.4 = ((bf16[8,384,768]{2,1,0:T(8,128)(2,1)}), bf16[8,384,768]{2,1,0:T(8,128)(2,1)}, u32[]{:S(2)}, u32[]{:S(2)}) async-start(bf16[8,384,768]{2,1,0:T(8,128)(2,1)} %bitcast.363), calls=%async_computation.4 | async-start | bytes 9437184 | tf_op jit(solution)/shard_map/all_to_all | solution.py:185
  252.7 108.5 %all-to-all-start.2 = ((bf16[8,384,768]{2,1,0:T(8,128)(2,1)}), bf16[8,384,768]{2,1,0:T(8,128)(2,1)}, u32[]{:S(2)}, u32[]{:S(2)}) async-start(bf16[8,384,768]{2,1,0:T(8,128)(2,1)} %bitcast.366), calls=%async_computation.2 | async-start | bytes 9437184 | tf_op jit(solution)/shard_map/all_to_all | solution.py:157
  361.2 108.5 %all-to-all-start = ((bf16[8,384,768]{2,1,0:T(8,128)(2,1)}), bf16[8,384,768]{2,1,0:T(8,128)(2,1)}, u32[]{:S(2)}, u32[]{:S(2)}) async-start(bf16[8,384,768]{2,1,0:T(8,128)(2,1)} %bitcast.364), calls=%async_computation | async-start | bytes 9437184 | tf_op jit(solution)/shard_map/all_to_all | solution.py:157
  469.6 108.3 %all-to-all-start.6 = ((bf16[8,384,768]{2,1,0:T(8,128)(2,1)}), bf16[8,384,768]{2,1,0:T(8,128)(2,1)}, u32[]{:S(2)}, u32[]{:S(2)}) async-start(bf16[8,384,768]{2,1,0:T(8,128)(2,1)} %bitcast.365), calls=%async_computation.6 | async-start | bytes 9437184 | tf_op jit(solution)/shard_map/all_to_all | solution.py:185
  474.3 447.0 %all-reduce.26.cloned.1.call-start = ((), (), s32[]{:S(2)}) async-start(), calls=%async_computation.14 | async-start | bytes 37748736 | tf_op jit(solution)/shard_map/psum | solution.py:165
  482.0 17.7 %copy-start.152 = (bf16[3072,768]{1,0:T(8,128)(2,1)}, bf16[3072,768]{1,0:T(8,128)(2,1)S(1)}, u32[]{:S(2)}) copy-start(bf16[3072,768]{1,0:T(8,128)(2,1)S(1)} %get-tuple-element.139) | copy-start | bytes 14155780
  617.1 33.9 %copy-start.34 = (f32[768,768]{1,0:T(8,128)S(1)}, f32[768,768]{1,0:T(8,128)}, u32[]{:S(2)}) copy-start(f32[768,768]{1,0:T(8,128)} %copy-done.33) | copy-start | bytes 7077892
  618.3 61.5 %all-to-all-start.8 = ((bf16[8,2,36864]{2,1,0:T(2,128)(2,1)}), bf16[8,2,36864]{2,1,0:T(2,128)(2,1)}, u32[]{:S(2)}, u32[]{:S(2)}) async-start(bf16[8,2,36864]{2,1,0:T(2,128)(2,1)} %reshape.916), calls=%async_computation.8 | async-start | bytes 2359296 | tf_op jit(solution)/shard_map/all_to_all | solution.py:270
  921.3 110.1 %copy-start.38 = (bf16[8,384,768]{2,1,0:T(8,128)(2,1)S(1)}, bf16[8,384,768]{2,1,0:T(8,128)(2,1)}, u32[]{:S(2)}) copy-start(bf16[8,384,768]{2,1,0:T(8,128)(2,1)} %get-tuple-element.100) | copy-start | bytes 14155780
  921.3 217.8 %slice-start.8 = ((s8[4718592]{0:T(1024)(128)(4,1)}), s8[4194304]{0:T(1024)(128)(4,1)S(1)}, s32[]{:S(2)}) async-start(s8[4718592]{0:T(1024)(128)(4,1)} %bitcast.378), calls=%async_computation.23 | async-start | bytes 8388608
  1031.4 107.6 %slice-start.9 = ((s8[4718592]{0:T(1024)(128)(4,1)}), s8[524288]{0:T(1024)(128)(4,1)S(1)}, s32[]{:S(2)}) async-start(s8[4718592]{0:T(1024)(128)(4,1)} %bitcast.378), calls=%async_computation.24 | async-start | bytes 1048576
  1246.5 108.2 %all-to-all-start.3 = ((bf16[8,384,768]{2,1,0:T(8,128)(2,1)}), bf16[8,384,768]{2,1,0:T(8,128)(2,1)}, u32[]{:S(2)}, u32[]{:S(2)}) async-start(bf16[8,384,768]{2,1,0:T(8,128)(2,1)} %get-tuple-element.98), calls=%async_computation.3 | async-start | bytes 9437184 | tf_op jit(solution)/shard_map/all_to_all | solution.py:166
  1251.3 310.9 %all-reduce.24.cloned.1.call-start = ((), (), s32[]{:S(2)}) async-start(), calls=%async_computation.13 | async-start | bytes 4718592 | tf_op jit(solution)/shard_map/psum | solution.py:255
  1406.4 14.9 copy-start.71
  1406.4 14.9 copy-start.84
  1406.4 14.9 copy-start.97
  1406.4 16.3 copy-start.24
  1507.5 139.3 %all-reduce.22.cloned.1.call-start = ((), (), s32[]{:S(2)}) async-start(), calls=%async_computation.12 | async-start | bytes 2359296 | tf_op jit(solution)/shard_map/psum | solution.py:263
  (150 other events, 595.5 us)
Sparse Core Ops, SparseCore 0:
  24.3 40.3 all-reduce.17
  77.7 37.7 all-reduce.19
  601.2 320.0 all-reduce.25
  1507.6 54.4 all-reduce.23
  1566.1 80.6 all-reduce.21
where the time goes:
time: 1680 us; the launch traced here: 1670 us
  waiting for transfers between devices  693 us (41%)
  blocking collectives  397 us (24%)
  local copies, waits for them, and re-layouts  221 us (13%)
  other arithmetic  160 us (10%)
  matrix products  120 us (7%)
  starting transfers between devices  57.9 us (3%)
    all_to_all x2, blocking collectives, shards(): lax.all_to_all(in_summed.reshape(expert_count, capacity, feat_width), 'ex...  215 us
    psum x1, waiting for transfers between devices, shards(): summed = lax.psum(slice_out.astype(jnp.bfloat16), 'hidden')  209 us
    all_to_all x2, waiting for transfers between devices, shards(): lax.all_to_all(send_rows, 'expert', split_axis=0, concat_axis=0, tiled=True)  162 us
    all_to_all x2, waiting for transfers between devices, shards(): lax.all_to_all(send_grad, 'expert', split_axis=0, concat_axis=0, tiled=True)  141 us
    all_to_all x1, blocking collectives, shards(): lax.all_to_all(summed.reshape(expert_count, capacity, feat_width), 'exper...  110 us
    all_to_all x1, waiting for transfers between devices, shards(): lax.all_to_all(summed.reshape(expert_count, capacity, feat_width), 'exper...  58.5 us
    psum x1, waiting for transfers between devices, shards(): lax.psum(normed1_term.astype(jnp.bfloat16), 'hidden').astype(jnp.float32)  47.2 us
    psum x1, blocking collectives, shards(): lax.psum(gain1_total.astype(jnp.bfloat16), 'expert').astype(jnp.float32)  38.8 us
  transfers between devices with their start and end apart: 11, of which 11 were waited for; matrix products, arithmetic and copies ran while one was open for 15% of the time, Pallas kernels for 0%

commit v1 on v0

--- a/solution.py
+++ b/solution.py
@@ -252,7 +252,9 @@
         normed1_term = jnp.einsum(
             "crf,cdf->rd", qkv_grad, qkv_weight, preferred_element_type=jnp.float32
         )
-        normed1_grad = lax.psum(normed1_term.astype(jnp.bfloat16), "hidden").astype(jnp.float32)
+        normed1_grad = jnp.sum(
+            lax.all_gather(normed1_term.astype(jnp.bfloat16), "hidden"), axis=0
+        ).astype(jnp.float32)
         input_grad, gain1_grad, bias1_grad = norm1_pull(normed1_grad)
         gain1_total = gain1_total + gain1_grad
         bias1_total = bias1_total + bias1_grad

time: 1680 us -> 1760 us (1.048)
  waiting for transfers between devices: 693 us -> 787 us
  blocking collectives: 397 us -> 364 us
    psum x1, waiting for transfers between devices: 209 us -> 320 us  [shards(): summed = lax.psum(slice_out.astype(jnp.bfloat16), 'hidden')]
    psum x1 -> x0, waiting for transfers between devices: 47.2 us -> none  [shards(): lax.psum(normed1_term.astype(jnp.bfloat16), 'hidden').astype(jnp.float32)]
    all_to_all x1 -> x0, blocking collectives: 32.5 us -> none  [shards(): lax.all_to_all(expert_acc[1][None].astype(jnp.bfloat16), 'expert', split_...]
    psum x1, waiting for transfers between devices: 29 us -> 0.01 us  [shards(): lax.psum(grad_qkv.astype(jnp.bfloat16), 'expert').astype(jnp.float32)]
    all_to_all x0 -> x1, waiting for transfers between devices: none -> 19.2 us  [shards(): lax.all_to_all(expert_acc[1][None].astype(jnp.bfloat16), 'expert', split_...]
  transfers between devices with their start and end apart: 11 -> 13, of which waited for: 11 -> 11; matrix products, arithmetic and copies ran while one was open for 15% -> 15% of each run, Pallas kernels for 0% -> 0%
where the time goes in v1:
time: 1760 us; the launch traced here: 1750 us
  waiting for transfers between devices  787 us (45%)
  blocking collectives  364 us (21%)
  local copies, waits for them, and re-layouts  225 us (13%)
  other arithmetic  171 us (10%)
  matrix products  120 us (7%)
  starting transfers between devices  64.8 us (4%)
    psum x1, waiting for transfers between devices, shards(): summed = lax.psum(slice_out.astype(jnp.bfloat16), 'hidden')  320 us
    all_to_all x2, blocking collectives, shards(): lax.all_to_all(in_summed.reshape(expert_count, capacity, feat_width), 'ex...  215 us
    all_to_all x2, waiting for transfers between devices, shards(): lax.all_to_all(send_rows, 'expert', split_axis=0, concat_axis=0, tiled=True)  162 us
    all_to_all x2, waiting for transfers between devices, shards(): lax.all_to_all(send_grad, 'expert', split_axis=0, concat_axis=0, tiled=True)  141 us
    all_to_all x1, blocking collectives, shards(): lax.all_to_all(summed.reshape(expert_count, capacity, feat_width), 'exper...  110 us
    all_to_all x1, waiting for transfers between devices, shards(): lax.all_to_all(summed.reshape(expert_count, capacity, feat_width), 'exper...  73.2 us
    psum x1, blocking collectives, shards(): lax.psum(gain1_total.astype(jnp.bfloat16), 'expert').astype(jnp.float32)  38.4 us
    all_to_all x1, starting transfers between devices, shards(): lax.all_to_all(expert_acc[0][None].astype(jnp.bfloat16), 'expert', split_...  36 us
  transfers between devices with their start and end apart: 13, of which 11 were waited for; matrix products, arithmetic and copies ran while one was open for 15% of the time, Pallas kernels for 0%

profile of v1, /device:TPU:0, one launch (start us, length us, event | category | flops | bytes accessed | tf_op | source)
XLA Modules:
  0.0 1748.3 jit_solution(1707819426683097036)
XLA Ops:
  46.4 18.2 %all-reduce.16.cloned.1.call-done = bf16[768,768]{1,0:T(8,128)(2,1)} async-done(((bf16[768,768]{1,0:T(8,128)(2,1)}), bf16[768,768]{1,0:T(8,128)(2,1)}) %all-reduce.16.cloned.1.call-update) | async-done | bytes 1179664 | tf_op jit(solution)/shard_map/psum | solution.py:143
  128.1 14.5 gather_fusion.4
  159.8 14.5 gather_fusion.2
  174.4 78.2 %all-to-all-done.4 = bf16[8,384,768]{2,1,0:T(8,128)(2,1)} async-done(((bf16[8,384,768]{2,1,0:T(8,128)(2,1)}), bf16[8,384,768]{2,1,0:T(8,128)(2,1)}, u32[]{:S(2)}, u32[]{:S(2)}) %all-to-all-start.4) | async-done | bytes 4718624 | tf_op jit(solution)/shard_map/all_to_all | solution.py:185
  257.5 14.5 gather_fusion
  272.0 89.1 %all-to-all-done.2 = bf16[8,384,768]{2,1,0:T(8,128)(2,1)} async-done(((bf16[8,384,768]{2,1,0:T(8,128)(2,1)}), bf16[8,384,768]{2,1,0:T(8,128)(2,1)}, u32[]{:S(2)}, u32[]{:S(2)}) %all-to-all-start.2) | async-done | bytes 4718624 | tf_op jit(solution)/shard_map/all_to_all | solution.py:157
  382.1 14.6 gather_fusion.6
  396.7 72.9 %all-to-all-done = bf16[8,384,768]{2,1,0:T(8,128)(2,1)} async-done(((bf16[8,384,768]{2,1,0:T(8,128)(2,1)}), bf16[8,384,768]{2,1,0:T(8,128)(2,1)}, u32[]{:S(2)}, u32[]{:S(2)}) %all-to-all-start) | async-done | bytes 4718624 | tf_op jit(solution)/shard_map/all_to_all | solution.py:157
  481.8 12.1 fusion.6
  505.0 10.1 multiply_convert_fusion
  515.1 62.8 %all-to-all-done.6 = bf16[8,384,768]{2,1,0:T(8,128)(2,1)} async-done(((bf16[8,384,768]{2,1,0:T(8,128)(2,1)}), bf16[8,384,768]{2,1,0:T(8,128)(2,1)}, u32[]{:S(2)}, u32[]{:S(2)}) %all-to-all-start.6) | async-done | bytes 4718624 | tf_op jit(solution)/shard_map/all_to_all | solution.py:185
  577.9 12.1 fusion.13
  601.4 320.2 %all-reduce.22.cloned.1.call-done = (bf16[8,384,768]{2,1,0:T(8,128)(2,1)}, bf16[8,384,768]{2,1,0:T(8,128)(2,1)}, bf16[8,384,768]{2,1,0:T(8,128)(2,1)}, bf16[8,384,768]{2,1,0:T(8,128)(2,1)}) async-done(((bf16[8,384,768]{2,1,0:T(8,128)(2,1)}, bf16[8,384,768]{2,1,0:T(8,128)(2,1)}, bf16[8,384,768]{2,1,0:T(8,128)(2,1)}, bf16[8,384,768]{2,1,0:T(8,128)(2,1)}), (bf16[8,384,768]{2,1,0:T(8,128)(2,1)}, ...) | async-done | bytes 18874384 | tf_op jit(solution)/shard_map/psum | solution.py:165
  921.6 110.1 %all_to_all.58 = bf16[8,384,768]{2,1,0:T(8,128)(2,1)} all-to-all(bf16[8,384,768]{2,1,0:T(8,128)(2,1)} %get-tuple-element.97), channel_id=1, replica_groups=mesh['expert'=8,'hidden'=4] {'expert'}, dimensions={0} | all-to-all | bytes 9437184 | tf_op jit(solution)/shard_map/all_to_all | solution.py:166
  1031.7 107.6 %all_to_all.59 = bf16[8,384,768]{2,1,0:T(8,128)(2,1)} all-to-all(bf16[8,384,768]{2,1,0:T(8,128)(2,1)S(1)} %copy-done.33), channel_id=1, replica_groups=mesh['expert'=8,'hidden'=4] {'expert'}, dimensions={0} | all-to-all | bytes 9437184 | tf_op jit(solution)/shard_map/all_to_all | solution.py:193
  1139.3 107.5 %all_to_all.60 = bf16[8,384,768]{2,1,0:T(8,128)(2,1)} all-to-all(bf16[8,384,768]{2,1,0:T(8,128)(2,1)S(1)} %bitcast.383), channel_id=1, replica_groups=mesh['expert'=8,'hidden'=4] {'expert'}, dimensions={0} | all-to-all | bytes 9437184 | tf_op jit(solution)/shard_map/all_to_all | solution.py:193
  1281.9 73.2 %all-to-all-done.3 = bf16[8,384,768]{2,1,0:T(8,128)(2,1)} async-done(((bf16[8,384,768]{2,1,0:T(8,128)(2,1)}), bf16[8,384,768]{2,1,0:T(8,128)(2,1)}, u32[]{:S(2)}, u32[]{:S(2)}) %all-to-all-start.3) | async-done | bytes 4718624 | tf_op jit(solution)/shard_map/all_to_all | solution.py:166
  1385.7 13.4 multiply_reduce_fusion.2
  1406.4 13.4 multiply_reduce_fusion.3
  1527.4 36.0 %all-to-all-start.8 = ((bf16[8,2,36864]{2,1,0:T(2,128)(2,1)}), bf16[8,2,36864]{2,1,0:T(2,128)(2,1)}, u32[]{:S(2)}, u32[]{:S(2)}) async-start(bf16[8,2,36864]{2,1,0:T(2,128)(2,1)} %reshape.918), calls=%async_computation.8 | async-start | bytes 2359296 | tf_op jit(solution)/shard_map/all_to_all | solution.py:272
  1578.6 26.2 %all-to-all-done.8 = bf16[8,2,36864]{2,1,0:T(2,128)(2,1)} async-done(((bf16[8,2,36864]{2,1,0:T(2,128)(2,1)}), bf16[8,2,36864]{2,1,0:T(2,128)(2,1)}, u32[]{:S(2)}, u32[]{:S(2)}) %all-to-all-start.8) | async-done | bytes 1179680 | tf_op jit(solution)/shard_map/all_to_all | solution.py:272
  1618.2 19.2 %all-to-all-done.9 = bf16[8,2,36864]{2,1,0:T(2,128)(2,1)S(1)} async-done(((bf16[8,2,36864]{2,1,0:T(2,128)(2,1)}), bf16[8,2,36864]{2,1,0:T(2,128)(2,1)S(1)}, u32[]{:S(2)}, u32[]{:S(2)}) %all-to-all-start.9) | async-done | bytes 1179680 | tf_op jit(solution)/shard_map/all_to_all | solution.py:279
  1658.4 17.0 all-gather.7.cloned.1.call-done
  1687.3 38.4 %all-reduce.8 = (bf16[768]{0:T(1024)(128)(2,1)}, bf16[768]{0:T(1024)(128)(2,1)}, bf16[768]{0:T(1024)(128)(2,1)}, bf16[768]{0:T(1024)(128)(2,1)}, bf16[768,8]{0,1:T(8,128)(2,1)}) all-reduce(bf16[768]{0:T(1024)(128)(2,1)} %add_convert_fusion.6, ...), channel_id=1, replica_groups=mesh['expert'=8,'hidden'=4] {'expert'}, use_global_device_ids=true, to_apply=%region_56.57 | all-reduce | flops 9216 | bytes 36864 | tf_op jit(solution)/shard_map/psum | solution.py:263
  (530 shorter events, 438.9 us)
Async XLA Ops:
  7.2 467.1 %copy-start = (bf16[1,768,768]{2,1,0:T(8,128)(2,1)S(1)}, bf16[1,768,768]{2,1,0:T(8,128)(2,1)}, u32[]{:S(2)}) copy-start(bf16[1,768,768]{2,1,0:T(8,128)(2,1)} %param.29) | copy-start | bytes 3538948
  7.2 57.3 %all-reduce.16.cloned.1.call-start = ((), (), s32[]{:S(2)}) async-start(), calls=%async_computation.10 | async-start | bytes 2359296 | tf_op jit(solution)/shard_map/psum | solution.py:143
  24.1 91.3 %all-reduce.18.cloned.1.call-start = ((), (), s32[]{:S(2)}) async-start(), calls=%async_computation.11 | async-start | bytes 2359296 | tf_op jit(solution)/shard_map/psum | solution.py:143
  25.7 97.4 %copy-start.96 = (s32[768,2]{0,1:T(2,128)}, s32[768,2]{0,1:T(2,128)S(1)}, u32[]{:S(2)}) copy-start(s32[768,2]{0,1:T(2,128)S(1)} %get-tuple-element.123) | copy-start | bytes 18436
  42.2 25.1 %copy-start.82 = (f32[768]{0:T(1024)}, f32[768]{0:T(1024)S(1)}, u32[]{:S(2)}) copy-start(f32[768]{0:T(1024)S(1)} %broadcast_multiply_fusion.3) | copy-start | bytes 9220
  88.0 17.5 copy-start.133
  105.5 13.8 copy-start.92
  142.7 110.0 %all-to-all-start.4 = ((bf16[8,384,768]{2,1,0:T(8,128)(2,1)}), bf16[8,384,768]{2,1,0:T(8,128)(2,1)}, u32[]{:S(2)}, u32[]{:S(2)}) async-start(bf16[8,384,768]{2,1,0:T(8,128)(2,1)} %bitcast.365), calls=%async_computation.4 | async-start | bytes 9437184 | tf_op jit(solution)/shard_map/all_to_all | solution.py:185
  252.6 108.5 %all-to-all-start.2 = ((bf16[8,384,768]{2,1,0:T(8,128)(2,1)}), bf16[8,384,768]{2,1,0:T(8,128)(2,1)}, u32[]{:S(2)}, u32[]{:S(2)}) async-start(bf16[8,384,768]{2,1,0:T(8,128)(2,1)} %bitcast.368), calls=%async_computation.2 | async-start | bytes 9437184 | tf_op jit(solution)/shard_map/all_to_all | solution.py:157
  361.1 108.5 %all-to-all-start = ((bf16[8,384,768]{2,1,0:T(8,128)(2,1)}), bf16[8,384,768]{2,1,0:T(8,128)(2,1)}, u32[]{:S(2)}, u32[]{:S(2)}) async-start(bf16[8,384,768]{2,1,0:T(8,128)(2,1)} %bitcast.366), calls=%async_computation | async-start | bytes 9437184 | tf_op jit(solution)/shard_map/all_to_all | solution.py:157
  469.6 108.3 %all-to-all-start.6 = ((bf16[8,384,768]{2,1,0:T(8,128)(2,1)}), bf16[8,384,768]{2,1,0:T(8,128)(2,1)}, u32[]{:S(2)}, u32[]{:S(2)}) async-start(bf16[8,384,768]{2,1,0:T(8,128)(2,1)} %bitcast.367), calls=%async_computation.6 | async-start | bytes 9437184 | tf_op jit(solution)/shard_map/all_to_all | solution.py:185
  474.2 447.4 %all-reduce.22.cloned.1.call-start = ((), (), s32[]{:S(2)}) async-start(), calls=%async_computation.15 | async-start | bytes 37748736 | tf_op jit(solution)/shard_map/psum | solution.py:165
  481.8 17.6 %copy-start.148 = (bf16[3072,768]{1,0:T(8,128)(2,1)}, bf16[3072,768]{1,0:T(8,128)(2,1)S(1)}, u32[]{:S(2)}) copy-start(bf16[3072,768]{1,0:T(8,128)(2,1)S(1)} %get-tuple-element.137) | copy-start | bytes 14155780
  921.6 110.1 %copy-start.33 = (bf16[8,384,768]{2,1,0:T(8,128)(2,1)S(1)}, bf16[8,384,768]{2,1,0:T(8,128)(2,1)}, u32[]{:S(2)}) copy-start(bf16[8,384,768]{2,1,0:T(8,128)(2,1)} %get-tuple-element.98) | copy-start | bytes 14155780
  921.6 217.8 %slice-start.8 = ((s8[4718592]{0:T(1024)(128)(4,1)}), s8[4194304]{0:T(1024)(128)(4,1)S(1)}, s32[]{:S(2)}) async-start(s8[4718592]{0:T(1024)(128)(4,1)} %bitcast.382), calls=%async_computation.24 | async-start | bytes 8388608
  1031.7 107.6 %slice-start.9 = ((s8[4718592]{0:T(1024)(128)(4,1)}), s8[524288]{0:T(1024)(128)(4,1)S(1)}, s32[]{:S(2)}) async-start(s8[4718592]{0:T(1024)(128)(4,1)} %bitcast.382), calls=%async_computation.25 | async-start | bytes 1048576
  1246.8 108.3 %all-to-all-start.3 = ((bf16[8,384,768]{2,1,0:T(8,128)(2,1)}), bf16[8,384,768]{2,1,0:T(8,128)(2,1)}, u32[]{:S(2)}, u32[]{:S(2)}) async-start(bf16[8,384,768]{2,1,0:T(8,128)(2,1)} %get-tuple-element.96), calls=%async_computation.3 | async-start | bytes 9437184 | tf_op jit(solution)/shard_map/all_to_all | solution.py:166
  1251.6 398.7 %all-reduce.20.cloned.1.call-start = ((), (), s32[]{:S(2)}) async-start(), calls=%async_computation.14 | async-start | bytes 2359296 | tf_op jit(solution)/shard_map/psum | solution.py:265
  1479.4 15.1 copy-start.94
  1501.4 153.2 %all-gather.5.cloned.1.call-start = ((), (), s32[]{:S(2)}) async-start(), calls=%async_computation.12 | async-start | bytes 5898240 | tf_op jit(solution)/shard_map/all_gather | solution.py:256
  1505.0 170.5 %all-gather.7.cloned.1.call-start = ((), (), s32[]{:S(2)}) async-start(), calls=%async_computation.13 | async-start | bytes 5898240 | tf_op jit(solution)/shard_map/all_gather | solution.py:256
  1527.4 77.3 %all-to-all-start.8 = ((bf16[8,2,36864]{2,1,0:T(2,128)(2,1)}), bf16[8,2,36864]{2,1,0:T(2,128)(2,1)}, u32[]{:S(2)}, u32[]{:S(2)}) async-start(bf16[8,2,36864]{2,1,0:T(2,128)(2,1)} %reshape.918), calls=%async_computation.8 | async-start | bytes 2359296 | tf_op jit(solution)/shard_map/all_to_all | solution.py:272
  1604.8 32.7 %all-to-all-start.9 = ((bf16[8,2,36864]{2,1,0:T(2,128)(2,1)}), bf16[8,2,36864]{2,1,0:T(2,128)(2,1)S(1)}, u32[]{:S(2)}, u32[]{:S(2)}) async-start(bf16[8,2,36864]{2,1,0:T(2,128)(2,1)} %reshape.920), calls=%async_computation.9 | async-start | bytes 2359296 | tf_op jit(solution)/shard_map/all_to_all | solution.py:279
  1683.3 50.1 %copy-start.95 = (f32[768]{0:T(1024)S(1)}, f32[768]{0:T(1024)}, u32[]{:S(2)}) copy-start(f32[768]{0:T(1024)} %copy-done.94) | copy-start | bytes 9220
  (148 other events, 629.1 us)
Sparse Core Ops, SparseCore 0:
  24.2 40.3 all-reduce.15
  77.6 37.7 all-reduce.17
  601.5 320.0 all-reduce.21
  1501.5 98.4 all-reduce.19
  1601.3 35.1 all-gather.4
  1638.0 37.4 all-gather.6
